TPU v7x, 32 devices: a whole 2x2x4 slice. The times are simulated.
32 devices in a mesh: block: 8 (over y, x, core), sub: 4 (over z).
Axes of the slice: x: 2, y: 2, z: 4, core: 2. Of those that a mesh axis runs over, the one named last changes fastest.
Arguments:
- source: float32 [8, 16, 128, 128], P('block', 'sub'), may hold values from -48 to 48
- trans_x: float32 [8, 16, 128, 128], P('block', 'sub'), may hold values from 0.1 to 10
- trans_y: float32 [8, 16, 128, 128], P('block', 'sub'), may hold values from 0.1 to 10
- trans_z: float32 [8, 16, 128, 128], P('block', 'sub'), may hold values from 0.1 to 10
- mortar_bot: float32 [8, 16, 128, 256], P('block', 'sub'), may hold values from -0.375 to 0.375
- mortar_top: float32 [8, 16, 128, 256], P('block', 'sub'), may hold values from -0.375 to 0.375
Outputs:
- pressure: float32 [8, 16, 128, 128], P('block', 'sub')
- mortar: float32 [8, 256], P('block', 'sub')
All inputs are finite; a program needn't handle non-finite values.
Results may differ from a plain program's by a relative error of at most 0.0003.
Values sent between devices are 32-bit elements; how exact they have to be, the bound alone decides.
No kernel may reach another device: no remote copies, remote signals or barrier semaphores. Data moves between devices by JAX's collectives and lax.ppermute only.
A program may use at most 64 MiB of HBM per device.

v0:
```python
import jax
import jax.numpy as jnp
from jax import lax
from jax.sharding import PartitionSpec as P

PASSES = 3
OUTER = 2
RELAX = 0.8
MORTAR_STEP = 0.05
HIGHEST = lax.Precision.HIGHEST


def from_behind(block, axis, distance):
    devices = range(lax.axis_size(axis))
    route = [(i - distance, i) for i in devices if i - distance in devices]
    return lax.ppermute(block, axis, route)


def with_halo(value, sides, width):
    for axis, dim in sides:
        devices, length = (lax.axis_size(axis), value.shape[dim])
        up = [(i, (i + 1) % devices) for i in range(devices - 1)]
        down = [(j, i) for i, j in up]
        last = lax.slice_in_dim(value, length - width, length, axis=dim)
        leading = lax.slice_in_dim(value, 0, width, axis=dim)
        before = lax.ppermute(last, axis, up)
        after = lax.ppermute(leading, axis, down)
        value = jnp.concatenate([before, value, after], axis=dim)
    return value


def below_of(values, axis):
    widths = [(0, 0)] * values.ndim
    widths[axis] = (1, 0)
    return lax.slice_in_dim(jnp.pad(values, widths), 0, values.shape[axis], axis=axis)


def above_of(values, axis):
    widths = [(0, 0)] * values.ndim
    widths[axis] = (0, 1)
    return lax.slice_in_dim(jnp.pad(values, widths), 1, values.shape[axis] + 1, axis=axis)


def widen_one(values):
    return jnp.pad(values, ((0, 0), (1, 1), (0, 0), (0, 0)))


def relax_pass(padded, rhs_part, offset, coeffs):
    coupling_x, coupling_next, coupling_y, coupling_z, diagonal = coeffs
    count = padded.shape[1] - 2

    def window(values):
        return values[:, offset : offset + count]

    centre = padded[:, 1:-1]
    part_x = window(coupling_x)
    part_next = window(coupling_next)
    part_y = window(coupling_y)
    part_z = window(coupling_z)
    part_diag = window(diagonal)
    applied = (
        part_diag * centre
        - part_x * padded[:, :-2]
        - part_next * padded[:, 2:]
        - part_y * below_of(centre, 2)
        - above_of(part_y, 2) * above_of(centre, 2)
        - part_z * below_of(centre, 3)
        - above_of(part_z, 3) * above_of(centre, 3)
    )
    return centre + RELAX * (rhs_part - applied) / part_diag


def shards(source, trans_x, trans_y, trans_z, mortar_bot, mortar_top):
    local_x = source.shape[1]
    rows_y = source.shape[2]
    cells_z = source.shape[3]
    mortars = mortar_bot.shape[3]
    sub_count = lax.axis_size("sub")
    block_count = lax.axis_size("block")
    sub_index = lax.axis_index("sub")
    block_index = lax.axis_index("block")
    share = mortars // sub_count
    depth = 1
    global_x = lax.broadcasted_iota(jnp.int32, source.shape, 1) + sub_index * local_x
    masked_x = jnp.where(global_x > 0, trans_x, 0.0)
    upper_layer = from_behind(masked_x[:, 0:1], "sub", -1)
    coupling_x = widen_one(masked_x)
    coupling_next = widen_one(jnp.concatenate([masked_x[:, 1:], upper_layer], axis=1))
    raw_y = widen_one(trans_y)
    raw_z = widen_one(trans_z)
    wide_shape = coupling_x.shape
    wide_x = lax.broadcasted_iota(jnp.int32, wide_shape, 1) - depth + sub_index * local_x
    index_y = lax.broadcasted_iota(jnp.int32, wide_shape, 2)
    index_z = lax.broadcasted_iota(jnp.int32, wide_shape, 3)
    coupling_y = jnp.where(index_y > 0, raw_y, 0.0)
    coupling_z = jnp.where(index_z > 0, raw_z, 0.0)
    dirichlet_bot = jnp.where((index_z == 0) & (block_index > 0), raw_z, 0.0)
    dirichlet_top = jnp.where(
        (index_z == cells_z - 1) & (block_index < block_count - 1), raw_z, 0.0
    )
    diagonal = (
        coupling_x
        + coupling_next
        + coupling_y
        + above_of(coupling_y, 2)
        + coupling_z
        + above_of(coupling_z, 3)
        + dirichlet_bot
        + dirichlet_top
    )
    inside = (wide_x >= 0) & (wide_x < local_x * sub_count)
    diagonal = jnp.where(inside, diagonal, 1.0)
    coeffs = (coupling_x, coupling_next, coupling_y, coupling_z, diagonal)
    local_bot = dirichlet_bot[:, depth : depth + local_x]
    local_top = dirichlet_top[:, depth : depth + local_x]
    face_bot = mortar_bot.reshape(local_x * rows_y, mortars)
    face_top = mortar_top.reshape(local_x * rows_y, mortars)
    pressure = jnp.zeros_like(source)
    mortar_pair = jnp.zeros((2, mortars), jnp.float32)
    final_row = jnp.zeros((share,), jnp.float32)
    for outer_round in range(OUTER):
        bottom_data = jnp.dot(face_bot, mortar_pair[0], precision=HIGHEST).reshape(
            1, local_x, rows_y
        )
        top_data = jnp.dot(face_top, mortar_pair[1], precision=HIGHEST).reshape(1, local_x, rows_y)
        rhs = source + local_bot * bottom_data[..., None] + local_top * top_data[..., None]
        for pass_round in range(PASSES):
            padded = with_halo(pressure, (("sub", 1),), 1)
            pressure = relax_pass(padded, rhs, 1, coeffs)
        flux_bot = local_bot[..., 0] * (pressure[..., 0] - bottom_data)
        flux_top = local_top[..., cells_z - 1] * (pressure[..., cells_z - 1] - top_data)
        terms = jnp.stack(
            [
                jnp.dot(flux_bot.reshape(-1), face_bot, precision=HIGHEST),
                jnp.dot(flux_top.reshape(-1), face_top, precision=HIGHEST),
            ]
        )
        shares = lax.psum(terms, "sub")
        current_pair = mortar_pair
        nearby = with_halo(shares[None], (("block", 0),), 1)
        jumps = jnp.stack([nearby[0, 1] + nearby[1, 0], nearby[1, 1] + nearby[2, 0]])
        updated = current_pair + MORTAR_STEP * jumps
        mortar_pair = updated
        final_row = lax.dynamic_slice_in_dim(updated[1], sub_index * share, share, 0)
    return (pressure, final_row[None])


def solution(mesh):
    return jax.shard_map(
        shards,
        mesh=mesh,
        in_specs=(
            P("block", "sub", None, None),
            P("block", "sub", None, None),
            P("block", "sub", None, None),
            P("block", "sub", None, None),
            P("block", "sub", None, None),
            P("block", "sub", None, None),
        ),
        out_specs=(P("block", "sub", None, None), P("block", "sub")),
        check_vma=False,
    )
```

profile of v0, /device:TPU:12, one launch (start us, length us, event | category | flops | bytes accessed | tf_op | source)
XLA Modules:
  0.0 99.8 jit_solution(6974258271982418281)
XLA Ops:
  0.7 2.5 %collective-permute-start.2 = (f32[1,1,128,128]{2,1,3,0:T(1,128)S(1)}, f32[1,1,128,128]{2,1,3,0:T(1,128)S(1)}, u32[]{:S(2)}, u32[]{:S(2)}) collective-permute-start(f32[1,1,128,128]{2,1,3,0:T(1,128)S(1)} %broadcast.138), channel_id=1, source_target_pairs={{1,0},{2,1},{3,2},{5,4},{6,5},{7,6},{9,8},{10,9},{11,10},{13,12},{... | collective-permute-start | bytes 196616 | tf_op jit(solution)/shard_map/ppermute | solution.py:27
  3.2 3.5 %collective-permute-start.1 = (f32[1,1,128,128]{2,1,3,0:T(1,128)S(1)}, f32[1,1,128,128]{2,1,3,0:T(1,128)S(1)}, u32[]{:S(2)}, u32[]{:S(2)}) collective-permute-start(f32[1,1,128,128]{2,1,3,0:T(1,128)S(1)} %broadcast.138), channel_id=1, source_target_pairs={{0,1},{1,2},{2,3},{4,5},{5,6},{6,7},{8,9},{9,10},{10,11},{12,13},{... | collective-permute-start | bytes 196616 | tf_op jit(solution)/shard_map/ppermute | solution.py:26
  6.7 1.1 %copy.10 = f32[1,4,128,128]{2,1,3,0:T(4,128)S(1)} copy(f32[1,4,128,128]{3,2,1,0:T(8,128)} %param.7) | data formatting | bytes 524288 | tf_op args[1]
  8.0 2.4 %collective-permute-start = (f32[1,1,128,128]{2,1,3,0:T(1,128)S(1)}, f32[1,1,128,128]{2,1,3,0:T(1,128)S(1)}, u32[]{:S(2)}, u32[]{:S(2)}) collective-permute-start(f32[1,1,128,128]{2,1,3,0:T(1,128)S(1)} %slice.352), channel_id=1, source_target_pairs={{1,0},{2,1},{3,2},{5,4},{6,5},{7,6},{9,8},{10,9},{11,10},{13,12},{... | collective-permute-start | bytes 196616 | tf_op jit(solution)/shard_map/ppermute | solution.py:16
  14.3 0.8 pad_select_fusion.2
  15.6 1.0 %fusion.9 = (f32[1,4,128,128]{2,1,3,0:T(4,128)S(1)}, f32[1,4,128,128]{2,1,3,0:T(4,128)S(1)}, f32[1,4,128,128]{2,1,3,0:T(4,128)S(1)}) fusion(f32[1,4,128,128]{2,1,3,0:T(4,128)S(1)} %slice.355, f32[1,4,128,128]{2,1,3,0:T(4,128)S(1)} %broadcast_in_dim.23, f32[1,1,128,128]{2,1,3,0:T(1,128)S(1)} %collective-permute-done.1, ...), kind=kLoop, calls=%fused_computation.48 | loop fusion | flops 1835008 | bytes 4329480 | tf_op jit(solution)/shard_map/div | solution.py:70
  16.7 3.5 %collective-permute-start.3 = (f32[1,1,128,128]{2,1,3,0:T(1,128)S(1)}, f32[1,1,128,128]{2,1,3,0:T(1,128)S(1)}, u32[]{:S(2)}, u32[]{:S(2)}) collective-permute-start(f32[1,1,128,128]{2,1,3,0:T(1,128)S(1)} %get-tuple-element.23), channel_id=1, source_target_pairs={{0,1},{1,2},{2,3},{4,5},{5,6},{6,7},{8,9},{9,10},{10,11},{12,13},{... | collective-permute-start | bytes 196616 | tf_op jit(solution)/shard_map/ppermute | solution.py:26
  20.2 2.4 %collective-permute-start.4 = (f32[1,1,128,128]{2,1,3,0:T(1,128)S(1)}, f32[1,1,128,128]{2,1,3,0:T(1,128)S(1)}, u32[]{:S(2)}, u32[]{:S(2)}) collective-permute-start(f32[1,1,128,128]{2,1,3,0:T(1,128)S(1)} %get-tuple-element.24), channel_id=1, source_target_pairs={{1,0},{2,1},{3,2},{5,4},{6,5},{7,6},{9,8},{10,9},{11,10},{13,12},{... | collective-permute-start | bytes 196616 | tf_op jit(solution)/shard_map/ppermute | solution.py:27
  22.9 3.5 %collective-permute-done.4 = f32[1,1,128,128]{2,1,3,0:T(1,128)S(1)} collective-permute-done((f32[1,1,128,128]{2,1,3,0:T(1,128)S(1)}, f32[1,1,128,128]{2,1,3,0:T(1,128)S(1)}, u32[]{:S(2)}, u32[]{:S(2)}) %collective-permute-start.4) | collective-permute-done | bytes 65568 | tf_op jit(solution)/shard_map/ppermute | solution.py:27
  26.4 0.8 fusion.96
  27.3 3.5 %collective-permute-start.5 = (f32[1,1,128,128]{2,1,3,0:T(1,128)S(1)}, f32[1,1,128,128]{2,1,3,0:T(1,128)S(1)}, u32[]{:S(2)}, u32[]{:S(2)}) collective-permute-start(f32[1,1,128,128]{2,1,3,0:T(1,128)S(1)} %get-tuple-element.21), channel_id=1, source_target_pairs={{0,1},{1,2},{2,3},{4,5},{5,6},{6,7},{8,9},{9,10},{10,11},{12,13},{... | collective-permute-start | bytes 196616 | tf_op jit(solution)/shard_map/ppermute | solution.py:26
  30.8 2.4 %collective-permute-start.6 = (f32[1,1,128,128]{2,1,3,0:T(1,128)S(1)}, f32[1,1,128,128]{2,1,3,0:T(1,128)S(1)}, u32[]{:S(2)}, u32[]{:S(2)}) collective-permute-start(f32[1,1,128,128]{2,1,3,0:T(1,128)S(1)} %get-tuple-element.22), channel_id=1, source_target_pairs={{1,0},{2,1},{3,2},{5,4},{6,5},{7,6},{9,8},{10,9},{11,10},{13,12},{... | collective-permute-start | bytes 196616 | tf_op jit(solution)/shard_map/ppermute | solution.py:27
  33.5 3.5 %collective-permute-done.6 = f32[1,1,128,128]{2,1,3,0:T(1,128)S(1)} collective-permute-done((f32[1,1,128,128]{2,1,3,0:T(1,128)S(1)}, f32[1,1,128,128]{2,1,3,0:T(1,128)S(1)}, u32[]{:S(2)}, u32[]{:S(2)}) %collective-permute-start.6) | collective-permute-done | bytes 65568 | tf_op jit(solution)/shard_map/ppermute | solution.py:27
  36.9 0.8 fusion.91
  38.5 8.8 %psum.14 = f32[1,2,256]{2,1,0:T(2,128)S(1)} all-reduce(f32[1,2,256]{2,1,0:T(2,128)S(1)} %maximum_bitcast_fusion), channel_id=1, replica_groups=mesh['block'=8,'sub'=4] {'sub'}, use_global_device_ids=true, to_apply=%region_0.1 | all-reduce | flops 512 | bytes 4096 | tf_op jit(solution)/shard_map/psum | solution.py:138
  47.3 1.9 %collective-permute-start.8 = (f32[1,2,256]{2,1,0:T(2,128)S(1)}, f32[1,2,256]{2,1,0:T(2,128)S(1)}, u32[]{:S(2)}, u32[]{:S(2)}) collective-permute-start(f32[1,2,256]{2,1,0:T(2,128)S(1)} %psum.14), channel_id=1, source_target_pairs={{4,0},{8,4},{12,8},{16,12},{20,16},{24,20},{28,24},{5,1},{9,5},{13... | collective-permute-start | bytes 6152 | tf_op jit(solution)/shard_map/ppermute | solution.py:27
  49.2 2.4 %collective-permute-start.7 = (f32[1,2,256]{2,1,0:T(2,128)S(1)}, f32[1,2,256]{2,1,0:T(2,128)S(1)}, u32[]{:S(2)}, u32[]{:S(2)}) collective-permute-start(f32[1,2,256]{2,1,0:T(2,128)S(1)} %psum.14), channel_id=1, source_target_pairs={{0,4},{4,8},{8,12},{12,16},{16,20},{20,24},{24,28},{1,5},{5,9},{9,... | collective-permute-start | bytes 6152 | tf_op jit(solution)/shard_map/ppermute | solution.py:26
  51.7 1.9 %collective-permute-start.9 = (f32[1,1,128,128]{2,1,3,0:T(1,128)S(1)}, f32[1,1,128,128]{2,1,3,0:T(1,128)S(1)}, u32[]{:S(2)}, u32[]{:S(2)}) collective-permute-start(f32[1,1,128,128]{2,1,3,0:T(1,128)S(1)} %get-tuple-element.19), channel_id=1, source_target_pairs={{0,1},{1,2},{2,3},{4,5},{5,6},{6,7},{8,9},{9,10},{10,11},{12,13},{... | collective-permute-start | bytes 196616 | tf_op jit(solution)/shard_map/ppermute | solution.py:26
  53.6 3.9 %collective-permute-start.10 = (f32[1,1,128,128]{2,1,3,0:T(1,128)S(1)}, f32[1,1,128,128]{2,1,3,0:T(1,128)S(1)}, u32[]{:S(2)}, u32[]{:S(2)}) collective-permute-start(f32[1,1,128,128]{2,1,3,0:T(1,128)S(1)} %get-tuple-element.20), channel_id=1, source_target_pairs={{1,0},{2,1},{3,2},{5,4},{6,5},{7,6},{9,8},{10,9},{11,10},{13,12},{... | collective-permute-start | bytes 196616 | tf_op jit(solution)/shard_map/ppermute | solution.py:27
  58.7 1.7 %collective-permute-done.10 = f32[1,1,128,128]{2,1,3,0:T(1,128)S(1)} collective-permute-done((f32[1,1,128,128]{2,1,3,0:T(1,128)S(1)}, f32[1,1,128,128]{2,1,3,0:T(1,128)S(1)}, u32[]{:S(2)}, u32[]{:S(2)}) %collective-permute-start.10) | collective-permute-done | bytes 65568 | tf_op jit(solution)/shard_map/ppermute | solution.py:27
  60.4 0.9 fusion.86
  61.4 3.1 %collective-permute-start.11 = (f32[1,1,128,128]{2,1,3,0:T(1,128)S(1)}, f32[1,1,128,128]{2,1,3,0:T(1,128)S(1)}, u32[]{:S(2)}, u32[]{:S(2)}) collective-permute-start(f32[1,1,128,128]{2,1,3,0:T(1,128)S(1)} %get-tuple-element.15), channel_id=1, source_target_pairs={{0,1},{1,2},{2,3},{4,5},{5,6},{6,7},{8,9},{9,10},{10,11},{12,13},{... | collective-permute-start | bytes 196616 | tf_op jit(solution)/shard_map/ppermute | solution.py:26
  64.5 2.8 %collective-permute-start.12 = (f32[1,1,128,128]{2,1,3,0:T(1,128)S(1)}, f32[1,1,128,128]{2,1,3,0:T(1,128)S(1)}, u32[]{:S(2)}, u32[]{:S(2)}) collective-permute-start(f32[1,1,128,128]{2,1,3,0:T(1,128)S(1)} %get-tuple-element.16), channel_id=1, source_target_pairs={{1,0},{2,1},{3,2},{5,4},{6,5},{7,6},{9,8},{10,9},{11,10},{13,12},{... | collective-permute-start | bytes 196616 | tf_op jit(solution)/shard_map/ppermute | solution.py:27
  67.6 3.1 %collective-permute-done.12 = f32[1,1,128,128]{2,1,3,0:T(1,128)S(1)} collective-permute-done((f32[1,1,128,128]{2,1,3,0:T(1,128)S(1)}, f32[1,1,128,128]{2,1,3,0:T(1,128)S(1)}, u32[]{:S(2)}, u32[]{:S(2)}) %collective-permute-start.12) | collective-permute-done | bytes 65568 | tf_op jit(solution)/shard_map/ppermute | solution.py:27
  71.6 1.9 %collective-permute-start.13 = (f32[1,1,128,128]{2,1,3,0:T(1,128)S(1)}, f32[1,1,128,128]{2,1,3,0:T(1,128)S(1)}, u32[]{:S(2)}, u32[]{:S(2)}) collective-permute-start(f32[1,1,128,128]{2,1,3,0:T(1,128)S(1)} %get-tuple-element.13), channel_id=1, source_target_pairs={{0,1},{1,2},{2,3},{4,5},{5,6},{6,7},{8,9},{9,10},{10,11},{12,13},{... | collective-permute-start | bytes 196616 | tf_op jit(solution)/shard_map/ppermute | solution.py:26
  73.5 3.9 %collective-permute-start.14 = (f32[1,1,128,128]{2,1,3,0:T(1,128)S(1)}, f32[1,1,128,128]{2,1,3,0:T(1,128)S(1)}, u32[]{:S(2)}, u32[]{:S(2)}) collective-permute-start(f32[1,1,128,128]{2,1,3,0:T(1,128)S(1)} %get-tuple-element.14), channel_id=1, source_target_pairs={{1,0},{2,1},{3,2},{5,4},{6,5},{7,6},{9,8},{10,9},{11,10},{13,12},{... | collective-permute-start | bytes 196616 | tf_op jit(solution)/shard_map/ppermute | solution.py:27
  77.7 1.9 %collective-permute-done.14 = f32[1,1,128,128]{2,1,3,0:T(1,128)S(1)} collective-permute-done((f32[1,1,128,128]{2,1,3,0:T(1,128)S(1)}, f32[1,1,128,128]{2,1,3,0:T(1,128)S(1)}, u32[]{:S(2)}, u32[]{:S(2)}) %collective-permute-start.14) | collective-permute-done | bytes 65568 | tf_op jit(solution)/shard_map/ppermute | solution.py:27
  81.1 10.3 %psum.15 = f32[1,2,256]{2,1,0:T(2,128)S(1)} all-reduce(f32[1,2,256]{2,1,0:T(2,128)S(1)} %maximum_bitcast_fusion.1), channel_id=1, replica_groups=mesh['block'=8,'sub'=4] {'sub'}, use_global_device_ids=true, to_apply=%region_1.2 | all-reduce | flops 512 | bytes 4096 | tf_op jit(solution)/shard_map/psum | solution.py:138
  91.5 1.9 %collective-permute-start.16 = (f32[1,2,256]{2,1,0:T(2,128)S(1)}, f32[1,2,256]{2,1,0:T(2,128)S(1)}, u32[]{:S(2)}, u32[]{:S(2)}) collective-permute-start(f32[1,2,256]{2,1,0:T(2,128)S(1)} %psum.15), channel_id=1, source_target_pairs={{4,0},{8,4},{12,8},{16,12},{20,16},{24,20},{28,24},{5,1},{9,5},{13... | collective-permute-start | bytes 6152 | tf_op jit(solution)/shard_map/ppermute | solution.py:27
  93.4 2.4 %collective-permute-start.15 = (f32[1,2,256]{2,1,0:T(2,128)S(1)}, f32[1,2,256]{2,1,0:T(2,128)S(1)}, u32[]{:S(2)}, u32[]{:S(2)}) collective-permute-start(f32[1,2,256]{2,1,0:T(2,128)S(1)} %psum.15), channel_id=1, source_target_pairs={{0,4},{4,8},{8,12},{12,16},{16,20},{20,24},{24,28},{1,5},{5,9},{9,... | collective-permute-start | bytes 6152 | tf_op jit(solution)/shard_map/ppermute | solution.py:26
  95.8 0.8 copy.13
  96.7 2.5 %collective-permute-done.15 = f32[1,2,256]{2,1,0:T(2,128)S(1)} collective-permute-done((f32[1,2,256]{2,1,0:T(2,128)S(1)}, f32[1,2,256]{2,1,0:T(2,128)S(1)}, u32[]{:S(2)}, u32[]{:S(2)}) %collective-permute-start.15) | collective-permute-done | bytes 2080 | tf_op jit(solution)/shard_map/ppermute | solution.py:26
  (71 shorter events, 10.9 us)
Async XLA Ops:
  0.6 10.5 %copy-start = (f32[1,4,128,256]{3,2,1,0:T(8,128)S(1)}, f32[1,4,128,256]{3,2,1,0:T(8,128)}, u32[]{:S(2)}) copy-start(f32[1,4,128,256]{3,2,1,0:T(8,128)} %param.10) | copy-start | bytes 1572868
  0.7 14.8 %collective-permute-start.2 = (f32[1,1,128,128]{2,1,3,0:T(1,128)S(1)}, f32[1,1,128,128]{2,1,3,0:T(1,128)S(1)}, u32[]{:S(2)}, u32[]{:S(2)}) collective-permute-start(f32[1,1,128,128]{2,1,3,0:T(1,128)S(1)} %broadcast.138), channel_id=1, source_target_pairs={{1,0},{2,1},{3,2},{5,4},{6,5},{7,6},{9,8},{10,9},{11,10},{13,12},{... | collective-permute-start | bytes 196616 | tf_op jit(solution)/shard_map/ppermute | solution.py:27
  3.2 12.4 %collective-permute-start.1 = (f32[1,1,128,128]{2,1,3,0:T(1,128)S(1)}, f32[1,1,128,128]{2,1,3,0:T(1,128)S(1)}, u32[]{:S(2)}, u32[]{:S(2)}) collective-permute-start(f32[1,1,128,128]{2,1,3,0:T(1,128)S(1)} %broadcast.138), channel_id=1, source_target_pairs={{0,1},{1,2},{2,3},{4,5},{5,6},{6,7},{8,9},{9,10},{10,11},{12,13},{... | collective-permute-start | bytes 196616 | tf_op jit(solution)/shard_map/ppermute | solution.py:26
  7.8 2.7 %copy-start.1 = (f32[1,4,128,256]{3,2,1,0:T(8,128)S(1)}, f32[1,4,128,256]{3,2,1,0:T(8,128)}, u32[]{:S(2)}) copy-start(f32[1,4,128,256]{3,2,1,0:T(8,128)} %param.11) | copy-start | bytes 1572868
  8.0 6.2 %collective-permute-start = (f32[1,1,128,128]{2,1,3,0:T(1,128)S(1)}, f32[1,1,128,128]{2,1,3,0:T(1,128)S(1)}, u32[]{:S(2)}, u32[]{:S(2)}) collective-permute-start(f32[1,1,128,128]{2,1,3,0:T(1,128)S(1)} %slice.352), channel_id=1, source_target_pairs={{1,0},{2,1},{3,2},{5,4},{6,5},{7,6},{9,8},{10,9},{11,10},{13,12},{... | collective-permute-start | bytes 196616 | tf_op jit(solution)/shard_map/ppermute | solution.py:16
  11.1 1.0 copy-start.6
  12.0 0.9 copy-start.7
  13.0 0.9 copy-start.8
  15.1 22.7 %copy-start.2 = (f32[1,6,128,128]{2,1,3,0:T(8,128)}, f32[1,6,128,128]{2,1,3,0:T(8,128)S(1)}, u32[]{:S(2)}) copy-start(f32[1,6,128,128]{2,1,3,0:T(8,128)S(1)} %get-tuple-element.25) | copy-start | bytes 1179652
  15.1 22.7 %copy-start.4 = (f32[1,6,128,128]{2,1,3,0:T(8,128)}, f32[1,6,128,128]{2,1,3,0:T(8,128)S(1)}, u32[]{:S(2)}) copy-start(f32[1,6,128,128]{2,1,3,0:T(8,128)S(1)} %get-tuple-element.26) | copy-start | bytes 1179652
  16.7 6.2 %collective-permute-start.3 = (f32[1,1,128,128]{2,1,3,0:T(1,128)S(1)}, f32[1,1,128,128]{2,1,3,0:T(1,128)S(1)}, u32[]{:S(2)}, u32[]{:S(2)}) collective-permute-start(f32[1,1,128,128]{2,1,3,0:T(1,128)S(1)} %get-tuple-element.23), channel_id=1, source_target_pairs={{0,1},{1,2},{2,3},{4,5},{5,6},{6,7},{8,9},{9,10},{10,11},{12,13},{... | collective-permute-start | bytes 196616 | tf_op jit(solution)/shard_map/ppermute | solution.py:26
  20.2 6.2 %collective-permute-start.4 = (f32[1,1,128,128]{2,1,3,0:T(1,128)S(1)}, f32[1,1,128,128]{2,1,3,0:T(1,128)S(1)}, u32[]{:S(2)}, u32[]{:S(2)}) collective-permute-start(f32[1,1,128,128]{2,1,3,0:T(1,128)S(1)} %get-tuple-element.24), channel_id=1, source_target_pairs={{1,0},{2,1},{3,2},{5,4},{6,5},{7,6},{9,8},{10,9},{11,10},{13,12},{... | collective-permute-start | bytes 196616 | tf_op jit(solution)/shard_map/ppermute | solution.py:27
  27.3 6.2 %collective-permute-start.5 = (f32[1,1,128,128]{2,1,3,0:T(1,128)S(1)}, f32[1,1,128,128]{2,1,3,0:T(1,128)S(1)}, u32[]{:S(2)}, u32[]{:S(2)}) collective-permute-start(f32[1,1,128,128]{2,1,3,0:T(1,128)S(1)} %get-tuple-element.21), channel_id=1, source_target_pairs={{0,1},{1,2},{2,3},{4,5},{5,6},{6,7},{8,9},{9,10},{10,11},{12,13},{... | collective-permute-start | bytes 196616 | tf_op jit(solution)/shard_map/ppermute | solution.py:26
  30.8 6.2 %collective-permute-start.6 = (f32[1,1,128,128]{2,1,3,0:T(1,128)S(1)}, f32[1,1,128,128]{2,1,3,0:T(1,128)S(1)}, u32[]{:S(2)}, u32[]{:S(2)}) collective-permute-start(f32[1,1,128,128]{2,1,3,0:T(1,128)S(1)} %get-tuple-element.22), channel_id=1, source_target_pairs={{1,0},{2,1},{3,2},{5,4},{6,5},{7,6},{9,8},{10,9},{11,10},{13,12},{... | collective-permute-start | bytes 196616 | tf_op jit(solution)/shard_map/ppermute | solution.py:27
  47.3 10.3 %collective-permute-start.8 = (f32[1,2,256]{2,1,0:T(2,128)S(1)}, f32[1,2,256]{2,1,0:T(2,128)S(1)}, u32[]{:S(2)}, u32[]{:S(2)}) collective-permute-start(f32[1,2,256]{2,1,0:T(2,128)S(1)} %psum.14), channel_id=1, source_target_pairs={{4,0},{8,4},{12,8},{16,12},{20,16},{24,20},{28,24},{5,1},{9,5},{13... | collective-permute-start | bytes 6152 | tf_op jit(solution)/shard_map/ppermute | solution.py:27
  49.2 8.4 %collective-permute-start.7 = (f32[1,2,256]{2,1,0:T(2,128)S(1)}, f32[1,2,256]{2,1,0:T(2,128)S(1)}, u32[]{:S(2)}, u32[]{:S(2)}) collective-permute-start(f32[1,2,256]{2,1,0:T(2,128)S(1)} %psum.14), channel_id=1, source_target_pairs={{0,4},{4,8},{8,12},{12,16},{16,20},{20,24},{24,28},{1,5},{5,9},{9,... | collective-permute-start | bytes 6152 | tf_op jit(solution)/shard_map/ppermute | solution.py:26
  51.7 7.0 %collective-permute-start.9 = (f32[1,1,128,128]{2,1,3,0:T(1,128)S(1)}, f32[1,1,128,128]{2,1,3,0:T(1,128)S(1)}, u32[]{:S(2)}, u32[]{:S(2)}) collective-permute-start(f32[1,1,128,128]{2,1,3,0:T(1,128)S(1)} %get-tuple-element.19), channel_id=1, source_target_pairs={{0,1},{1,2},{2,3},{4,5},{5,6},{6,7},{8,9},{9,10},{10,11},{12,13},{... | collective-permute-start | bytes 196616 | tf_op jit(solution)/shard_map/ppermute | solution.py:26
  53.6 6.7 %collective-permute-start.10 = (f32[1,1,128,128]{2,1,3,0:T(1,128)S(1)}, f32[1,1,128,128]{2,1,3,0:T(1,128)S(1)}, u32[]{:S(2)}, u32[]{:S(2)}) collective-permute-start(f32[1,1,128,128]{2,1,3,0:T(1,128)S(1)} %get-tuple-element.20), channel_id=1, source_target_pairs={{1,0},{2,1},{3,2},{5,4},{6,5},{7,6},{9,8},{10,9},{11,10},{13,12},{... | collective-permute-start | bytes 196616 | tf_op jit(solution)/shard_map/ppermute | solution.py:27
  57.6 2.7 %copy-start.3 = (f32[1,6,128,128]{2,1,3,0:T(8,128)S(1)}, f32[1,6,128,128]{2,1,3,0:T(8,128)}, u32[]{:S(2)}) copy-start(f32[1,6,128,128]{2,1,3,0:T(8,128)} %copy-done.2) | copy-start | bytes 1179652
  57.6 2.7 %copy-start.5 = (f32[1,6,128,128]{2,1,3,0:T(8,128)S(1)}, f32[1,6,128,128]{2,1,3,0:T(8,128)}, u32[]{:S(2)}) copy-start(f32[1,6,128,128]{2,1,3,0:T(8,128)} %copy-done.4) | copy-start | bytes 1179652
  61.4 6.2 %collective-permute-start.11 = (f32[1,1,128,128]{2,1,3,0:T(1,128)S(1)}, f32[1,1,128,128]{2,1,3,0:T(1,128)S(1)}, u32[]{:S(2)}, u32[]{:S(2)}) collective-permute-start(f32[1,1,128,128]{2,1,3,0:T(1,128)S(1)} %get-tuple-element.15), channel_id=1, source_target_pairs={{0,1},{1,2},{2,3},{4,5},{5,6},{6,7},{8,9},{9,10},{10,11},{12,13},{... | collective-permute-start | bytes 196616 | tf_op jit(solution)/shard_map/ppermute | solution.py:26
  64.5 6.2 %collective-permute-start.12 = (f32[1,1,128,128]{2,1,3,0:T(1,128)S(1)}, f32[1,1,128,128]{2,1,3,0:T(1,128)S(1)}, u32[]{:S(2)}, u32[]{:S(2)}) collective-permute-start(f32[1,1,128,128]{2,1,3,0:T(1,128)S(1)} %get-tuple-element.16), channel_id=1, source_target_pairs={{1,0},{2,1},{3,2},{5,4},{6,5},{7,6},{9,8},{10,9},{11,10},{13,12},{... | collective-permute-start | bytes 196616 | tf_op jit(solution)/shard_map/ppermute | solution.py:27
  71.6 6.2 %collective-permute-start.13 = (f32[1,1,128,128]{2,1,3,0:T(1,128)S(1)}, f32[1,1,128,128]{2,1,3,0:T(1,128)S(1)}, u32[]{:S(2)}, u32[]{:S(2)}) collective-permute-start(f32[1,1,128,128]{2,1,3,0:T(1,128)S(1)} %get-tuple-element.13), channel_id=1, source_target_pairs={{0,1},{1,2},{2,3},{4,5},{5,6},{6,7},{8,9},{9,10},{10,11},{12,13},{... | collective-permute-start | bytes 196616 | tf_op jit(solution)/shard_map/ppermute | solution.py:26
  73.5 6.2 %collective-permute-start.14 = (f32[1,1,128,128]{2,1,3,0:T(1,128)S(1)}, f32[1,1,128,128]{2,1,3,0:T(1,128)S(1)}, u32[]{:S(2)}, u32[]{:S(2)}) collective-permute-start(f32[1,1,128,128]{2,1,3,0:T(1,128)S(1)} %get-tuple-element.14), channel_id=1, source_target_pairs={{1,0},{2,1},{3,2},{5,4},{6,5},{7,6},{9,8},{10,9},{11,10},{13,12},{... | collective-permute-start | bytes 196616 | tf_op jit(solution)/shard_map/ppermute | solution.py:27
  91.5 5.2 %collective-permute-start.16 = (f32[1,2,256]{2,1,0:T(2,128)S(1)}, f32[1,2,256]{2,1,0:T(2,128)S(1)}, u32[]{:S(2)}, u32[]{:S(2)}) collective-permute-start(f32[1,2,256]{2,1,0:T(2,128)S(1)} %psum.15), channel_id=1, source_target_pairs={{4,0},{8,4},{12,8},{16,12},{20,16},{24,20},{28,24},{5,1},{9,5},{13... | collective-permute-start | bytes 6152 | tf_op jit(solution)/shard_map/ppermute | solution.py:27
  93.4 5.8 %collective-permute-start.15 = (f32[1,2,256]{2,1,0:T(2,128)S(1)}, f32[1,2,256]{2,1,0:T(2,128)S(1)}, u32[]{:S(2)}, u32[]{:S(2)}) collective-permute-start(f32[1,2,256]{2,1,0:T(2,128)S(1)} %psum.15), channel_id=1, source_target_pairs={{0,4},{4,8},{8,12},{12,16},{16,20},{20,24},{24,28},{1,5},{5,9},{9,... | collective-permute-start | bytes 6152 | tf_op jit(solution)/shard_map/ppermute | solution.py:26
where the time goes:
time: 100 us; the launch traced here: 99.8 us
  starting transfers between devices  46.2 us (46%)
  blocking collectives  19.1 us (19%)
  waiting for transfers between devices  17.4 us (17%)
  other arithmetic  7.05 us (7%)
  local copies, waits for them, and re-layouts  5.58 us (6%)
  matrix products  3.32 us (3%)
  between operations  1.12 us (1%)
    ppermute x8, starting transfers between devices, with_halo(): before = lax.ppermute(last, axis, up)  22.2 us
    ppermute x8, starting transfers between devices, with_halo(): after = lax.ppermute(leading, axis, down)  21.7 us
    psum x2, blocking collectives, shards(): shares = lax.psum(terms, 'sub')  19.1 us
    ppermute x8, waiting for transfers between devices, with_halo(): after = lax.ppermute(leading, axis, down)  13.7 us
    unnamed x23, local copies, waits for them, and re-layouts  4.42 us
    add x5, other arithmetic, relax_pass(): return centre + RELAX * (rhs_part - applied) / part_diag  4.21 us
    ppermute x8, waiting for transfers between devices, with_halo(): before = lax.ppermute(last, axis, up)  3.74 us
    ppermute x1, starting transfers between devices, from_behind(): return lax.ppermute(block, axis, route)  2.36 us
  transfers between devices with their start and end apart: 17, of which 10 were waited for; matrix products, arithmetic and copies ran while one was open for 6% of the time, Pallas kernels for 0%

commit v1 on v0

--- a/solution.py
+++ b/solution.py
@@ -135,7 +135,7 @@
                 jnp.dot(flux_top.reshape(-1), face_top, precision=HIGHEST),
             ]
         )
-        shares = lax.psum(terms, "sub")
+        shares = jnp.sum(lax.all_gather(terms, "sub"), axis=0)
         current_pair = mortar_pair
         nearby = with_halo(shares[None], (("block", 0),), 1)
         jumps = jnp.stack([nearby[0, 1] + nearby[1, 0], nearby[1, 1] + nearby[2, 0]])

time: 100 us -> 106 us (1.060)
  the two profiles are of different devices: /device:TPU:12 before, /device:TPU:4 now
where the time goes in v1:
time: 106 us; the launch traced here: 105 us
  starting transfers between devices  36.9 us (35%)
  waiting for transfers between devices  27.4 us (26%)
  blocking collectives  23.9 us (23%)
  other arithmetic  7.08 us (7%)
  local copies, waits for them, and re-layouts  5.58 us (5%)
  matrix products  3.32 us (3%)
  between operations  1.12 us (1%)
    all_gather x2, blocking collectives, shards(): shares = jnp.sum(lax.all_gather(terms, 'sub'), axis=0)  23.9 us
    ppermute x8, starting transfers between devices, with_halo(): before = lax.ppermute(last, axis, up)  23.9 us
    ppermute x8, waiting for transfers between devices, with_halo(): after = lax.ppermute(leading, axis, down)  21.4 us
    ppermute x8, starting transfers between devices, with_halo(): after = lax.ppermute(leading, axis, down)  11.7 us
    ppermute x8, waiting for transfers between devices, with_halo(): before = lax.ppermute(last, axis, up)  4.87 us
    unnamed x23, local copies, waits for them, and re-layouts  4.42 us
    add x5, other arithmetic, relax_pass(): return centre + RELAX * (rhs_part - applied) / part_diag  4.2 us
  transfers between devices with their start and end apart: 17, of which 11 were waited for; matrix products, arithmetic and copies ran while one was open for 6% of the time, Pallas kernels for 0%

profile of v1, /device:TPU:4, one launch (start us, length us, event | category | flops | bytes accessed | tf_op | source)
XLA Modules:
  0.0 105.2 jit_solution(12419961814943340151)
XLA Ops:
  0.7 1.4 %collective-permute-start.2 = (f32[1,1,128,128]{2,1,3,0:T(1,128)S(1)}, f32[1,1,128,128]{2,1,3,0:T(1,128)S(1)}, u32[]{:S(2)}, u32[]{:S(2)}) collective-permute-start(f32[1,1,128,128]{2,1,3,0:T(1,128)S(1)} %broadcast.138), channel_id=1, source_target_pairs={{1,0},{2,1},{3,2},{5,4},{6,5},{7,6},{9,8},{10,9},{11,10},{13,12},{... | collective-permute-start | bytes 196616 | tf_op jit(solution)/shard_map/ppermute | solution.py:27
  2.1 4.5 %collective-permute-start.1 = (f32[1,1,128,128]{2,1,3,0:T(1,128)S(1)}, f32[1,1,128,128]{2,1,3,0:T(1,128)S(1)}, u32[]{:S(2)}, u32[]{:S(2)}) collective-permute-start(f32[1,1,128,128]{2,1,3,0:T(1,128)S(1)} %broadcast.138), channel_id=1, source_target_pairs={{0,1},{1,2},{2,3},{4,5},{5,6},{6,7},{8,9},{9,10},{10,11},{12,13},{... | collective-permute-start | bytes 196616 | tf_op jit(solution)/shard_map/ppermute | solution.py:26
  6.7 1.1 %copy.16 = f32[1,4,128,128]{2,1,3,0:T(4,128)S(1)} copy(f32[1,4,128,128]{3,2,1,0:T(8,128)} %param.7) | data formatting | bytes 524288 | tf_op args[1]
  8.0 1.3 %collective-permute-start = (f32[1,1,128,128]{2,1,3,0:T(1,128)S(1)}, f32[1,1,128,128]{2,1,3,0:T(1,128)S(1)}, u32[]{:S(2)}, u32[]{:S(2)}) collective-permute-start(f32[1,1,128,128]{2,1,3,0:T(1,128)S(1)} %slice.352), channel_id=1, source_target_pairs={{1,0},{2,1},{3,2},{5,4},{6,5},{7,6},{9,8},{10,9},{11,10},{13,12},{... | collective-permute-start | bytes 196616 | tf_op jit(solution)/shard_map/ppermute | solution.py:16
  13.1 1.1 %collective-permute-done = f32[1,1,128,128]{2,1,3,0:T(1,128)S(1)} collective-permute-done((f32[1,1,128,128]{2,1,3,0:T(1,128)S(1)}, f32[1,1,128,128]{2,1,3,0:T(1,128)S(1)}, u32[]{:S(2)}, u32[]{:S(2)}) %collective-permute-start) | collective-permute-done | bytes 65568 | tf_op jit(solution)/shard_map/ppermute | solution.py:16
  15.6 1.0 fusion.9
  16.7 3.5 %collective-permute-start.3 = (f32[1,1,128,128]{2,1,3,0:T(1,128)S(1)}, f32[1,1,128,128]{2,1,3,0:T(1,128)S(1)}, u32[]{:S(2)}, u32[]{:S(2)}) collective-permute-start(f32[1,1,128,128]{2,1,3,0:T(1,128)S(1)} %get-tuple-element.25), channel_id=1, source_target_pairs={{0,1},{1,2},{2,3},{4,5},{5,6},{6,7},{8,9},{9,10},{10,11},{12,13},{... | collective-permute-start | bytes 196616 | tf_op jit(solution)/shard_map/ppermute | solution.py:26
  20.2 1.3 %collective-permute-start.4 = (f32[1,1,128,128]{2,1,3,0:T(1,128)S(1)}, f32[1,1,128,128]{2,1,3,0:T(1,128)S(1)}, u32[]{:S(2)}, u32[]{:S(2)}) collective-permute-start(f32[1,1,128,128]{2,1,3,0:T(1,128)S(1)} %get-tuple-element.26), channel_id=1, source_target_pairs={{1,0},{2,1},{3,2},{5,4},{6,5},{7,6},{9,8},{10,9},{11,10},{13,12},{... | collective-permute-start | bytes 196616 | tf_op jit(solution)/shard_map/ppermute | solution.py:27
  22.1 4.3 %collective-permute-done.4 = f32[1,1,128,128]{2,1,3,0:T(1,128)S(1)} collective-permute-done((f32[1,1,128,128]{2,1,3,0:T(1,128)S(1)}, f32[1,1,128,128]{2,1,3,0:T(1,128)S(1)}, u32[]{:S(2)}, u32[]{:S(2)}) %collective-permute-start.4) | collective-permute-done | bytes 65568 | tf_op jit(solution)/shard_map/ppermute | solution.py:27
  26.4 0.8 fusion.96
  27.3 3.5 %collective-permute-start.5 = (f32[1,1,128,128]{2,1,3,0:T(1,128)S(1)}, f32[1,1,128,128]{2,1,3,0:T(1,128)S(1)}, u32[]{:S(2)}, u32[]{:S(2)}) collective-permute-start(f32[1,1,128,128]{2,1,3,0:T(1,128)S(1)} %get-tuple-element.23), channel_id=1, source_target_pairs={{0,1},{1,2},{2,3},{4,5},{5,6},{6,7},{8,9},{9,10},{10,11},{12,13},{... | collective-permute-start | bytes 196616 | tf_op jit(solution)/shard_map/ppermute | solution.py:26
  30.8 1.3 %collective-permute-start.6 = (f32[1,1,128,128]{2,1,3,0:T(1,128)S(1)}, f32[1,1,128,128]{2,1,3,0:T(1,128)S(1)}, u32[]{:S(2)}, u32[]{:S(2)}) collective-permute-start(f32[1,1,128,128]{2,1,3,0:T(1,128)S(1)} %get-tuple-element.24), channel_id=1, source_target_pairs={{1,0},{2,1},{3,2},{5,4},{6,5},{7,6},{9,8},{10,9},{11,10},{13,12},{... | collective-permute-start | bytes 196616 | tf_op jit(solution)/shard_map/ppermute | solution.py:27
  32.7 4.3 %collective-permute-done.6 = f32[1,1,128,128]{2,1,3,0:T(1,128)S(1)} collective-permute-done((f32[1,1,128,128]{2,1,3,0:T(1,128)S(1)}, f32[1,1,128,128]{2,1,3,0:T(1,128)S(1)}, u32[]{:S(2)}, u32[]{:S(2)}) %collective-permute-start.6) | collective-permute-done | bytes 65568 | tf_op jit(solution)/shard_map/ppermute | solution.py:27
  37.0 0.8 fusion.91
  38.5 11.9 %all-gather.2 = f32[4,2,256]{2,1,0:T(2,128)S(1)} all-gather(f32[1,2,256]{2,1,0:T(2,128)S(1)} %maximum_bitcast_fusion), channel_id=2, replica_groups=mesh['block'=8,'sub'=4] {'sub'}, dimensions={0}, use_global_device_ids=true | all-gather | bytes 10240 | tf_op jit(solution)/shard_map/all_gather | solution.py:138
  50.4 1.9 %collective-permute-start.8 = (f32[1,2,256]{2,1,0:T(2,128)S(1)}, f32[1,2,256]{2,1,0:T(2,128)S(1)}, u32[]{:S(2)}, u32[]{:S(2)}) collective-permute-start(f32[1,2,256]{2,1,0:T(2,128)S(1)} %bitcast.117), channel_id=1, source_target_pairs={{4,0},{8,4},{12,8},{16,12},{20,16},{24,20},{28,24},{5,1},{9,5},{13... | collective-permute-start | bytes 6152 | tf_op jit(solution)/shard_map/ppermute | solution.py:27
  52.4 2.4 %collective-permute-start.7 = (f32[1,2,256]{2,1,0:T(2,128)S(1)}, f32[1,2,256]{2,1,0:T(2,128)S(1)}, u32[]{:S(2)}, u32[]{:S(2)}) collective-permute-start(f32[1,2,256]{2,1,0:T(2,128)S(1)} %bitcast.118), channel_id=1, source_target_pairs={{0,4},{4,8},{8,12},{12,16},{16,20},{20,24},{24,28},{1,5},{5,9},{9,... | collective-permute-start | bytes 6152 | tf_op jit(solution)/shard_map/ppermute | solution.py:26
  54.9 2.0 %collective-permute-start.9 = (f32[1,1,128,128]{2,1,3,0:T(1,128)S(1)}, f32[1,1,128,128]{2,1,3,0:T(1,128)S(1)}, u32[]{:S(2)}, u32[]{:S(2)}) collective-permute-start(f32[1,1,128,128]{2,1,3,0:T(1,128)S(1)} %get-tuple-element.21), channel_id=1, source_target_pairs={{0,1},{1,2},{2,3},{4,5},{5,6},{6,7},{8,9},{9,10},{10,11},{12,13},{... | collective-permute-start | bytes 196616 | tf_op jit(solution)/shard_map/ppermute | solution.py:26
  56.9 1.3 %collective-permute-start.10 = (f32[1,1,128,128]{2,1,3,0:T(1,128)S(1)}, f32[1,1,128,128]{2,1,3,0:T(1,128)S(1)}, u32[]{:S(2)}, u32[]{:S(2)}) collective-permute-start(f32[1,1,128,128]{2,1,3,0:T(1,128)S(1)} %get-tuple-element.22), channel_id=1, source_target_pairs={{1,0},{2,1},{3,2},{5,4},{6,5},{7,6},{9,8},{10,9},{11,10},{13,12},{... | collective-permute-start | bytes 196616 | tf_op jit(solution)/shard_map/ppermute | solution.py:27
  59.4 4.3 %collective-permute-done.10 = f32[1,1,128,128]{2,1,3,0:T(1,128)S(1)} collective-permute-done((f32[1,1,128,128]{2,1,3,0:T(1,128)S(1)}, f32[1,1,128,128]{2,1,3,0:T(1,128)S(1)}, u32[]{:S(2)}, u32[]{:S(2)}) %collective-permute-start.10) | collective-permute-done | bytes 65568 | tf_op jit(solution)/shard_map/ppermute | solution.py:27
  63.7 0.9 fusion.86
  64.7 3.3 %collective-permute-start.11 = (f32[1,1,128,128]{2,1,3,0:T(1,128)S(1)}, f32[1,1,128,128]{2,1,3,0:T(1,128)S(1)}, u32[]{:S(2)}, u32[]{:S(2)}) collective-permute-start(f32[1,1,128,128]{2,1,3,0:T(1,128)S(1)} %get-tuple-element.17), channel_id=1, source_target_pairs={{0,1},{1,2},{2,3},{4,5},{5,6},{6,7},{8,9},{9,10},{10,11},{12,13},{... | collective-permute-start | bytes 196616 | tf_op jit(solution)/shard_map/ppermute | solution.py:26
  68.0 1.3 %collective-permute-start.12 = (f32[1,1,128,128]{2,1,3,0:T(1,128)S(1)}, f32[1,1,128,128]{2,1,3,0:T(1,128)S(1)}, u32[]{:S(2)}, u32[]{:S(2)}) collective-permute-start(f32[1,1,128,128]{2,1,3,0:T(1,128)S(1)} %get-tuple-element.18), channel_id=1, source_target_pairs={{1,0},{2,1},{3,2},{5,4},{6,5},{7,6},{9,8},{10,9},{11,10},{13,12},{... | collective-permute-start | bytes 196616 | tf_op jit(solution)/shard_map/ppermute | solution.py:27
  69.9 4.3 %collective-permute-done.12 = f32[1,1,128,128]{2,1,3,0:T(1,128)S(1)} collective-permute-done((f32[1,1,128,128]{2,1,3,0:T(1,128)S(1)}, f32[1,1,128,128]{2,1,3,0:T(1,128)S(1)}, u32[]{:S(2)}, u32[]{:S(2)}) %collective-permute-start.12) | collective-permute-done | bytes 65568 | tf_op jit(solution)/shard_map/ppermute | solution.py:27
  75.1 2.2 %collective-permute-start.13 = (f32[1,1,128,128]{2,1,3,0:T(1,128)S(1)}, f32[1,1,128,128]{2,1,3,0:T(1,128)S(1)}, u32[]{:S(2)}, u32[]{:S(2)}) collective-permute-start(f32[1,1,128,128]{2,1,3,0:T(1,128)S(1)} %get-tuple-element.15), channel_id=1, source_target_pairs={{0,1},{1,2},{2,3},{4,5},{5,6},{6,7},{8,9},{9,10},{10,11},{12,13},{... | collective-permute-start | bytes 196616 | tf_op jit(solution)/shard_map/ppermute | solution.py:26
  77.3 1.3 %collective-permute-start.14 = (f32[1,1,128,128]{2,1,3,0:T(1,128)S(1)}, f32[1,1,128,128]{2,1,3,0:T(1,128)S(1)}, u32[]{:S(2)}, u32[]{:S(2)}) collective-permute-start(f32[1,1,128,128]{2,1,3,0:T(1,128)S(1)} %get-tuple-element.16), channel_id=1, source_target_pairs={{1,0},{2,1},{3,2},{5,4},{6,5},{7,6},{9,8},{10,9},{11,10},{13,12},{... | collective-permute-start | bytes 196616 | tf_op jit(solution)/shard_map/ppermute | solution.py:27
  79.2 4.3 %collective-permute-done.14 = f32[1,1,128,128]{2,1,3,0:T(1,128)S(1)} collective-permute-done((f32[1,1,128,128]{2,1,3,0:T(1,128)S(1)}, f32[1,1,128,128]{2,1,3,0:T(1,128)S(1)}, u32[]{:S(2)}, u32[]{:S(2)}) %collective-permute-start.14) | collective-permute-done | bytes 65568 | tf_op jit(solution)/shard_map/ppermute | solution.py:27
  85.0 11.9 %all-gather.3 = f32[4,2,256]{2,1,0:T(2,128)S(1)} all-gather(f32[1,2,256]{2,1,0:T(2,128)S(1)} %maximum_bitcast_fusion.1), channel_id=3, replica_groups=mesh['block'=8,'sub'=4] {'sub'}, dimensions={0}, use_global_device_ids=true | all-gather | bytes 10240 | tf_op jit(solution)/shard_map/all_gather | solution.py:138
  96.9 1.9 %collective-permute-start.16 = (f32[1,2,256]{2,1,0:T(2,128)S(1)}, f32[1,2,256]{2,1,0:T(2,128)S(1)}, u32[]{:S(2)}, u32[]{:S(2)}) collective-permute-start(f32[1,2,256]{2,1,0:T(2,128)S(1)} %bitcast.114), channel_id=1, source_target_pairs={{4,0},{8,4},{12,8},{16,12},{20,16},{24,20},{28,24},{5,1},{9,5},{13... | collective-permute-start | bytes 6152 | tf_op jit(solution)/shard_map/ppermute | solution.py:27
  98.8 2.4 %collective-permute-start.15 = (f32[1,2,256]{2,1,0:T(2,128)S(1)}, f32[1,2,256]{2,1,0:T(2,128)S(1)}, u32[]{:S(2)}, u32[]{:S(2)}) collective-permute-start(f32[1,2,256]{2,1,0:T(2,128)S(1)} %bitcast.115), channel_id=1, source_target_pairs={{0,4},{4,8},{8,12},{12,16},{16,20},{20,24},{24,28},{1,5},{5,9},{9,... | collective-permute-start | bytes 6152 | tf_op jit(solution)/shard_map/ppermute | solution.py:26
  101.3 0.8 copy.19
  102.1 2.5 %collective-permute-done.15 = f32[1,2,256]{2,1,0:T(2,128)S(1)} collective-permute-done((f32[1,2,256]{2,1,0:T(2,128)S(1)}, f32[1,2,256]{2,1,0:T(2,128)S(1)}, u32[]{:S(2)}, u32[]{:S(2)}) %collective-permute-start.15) | collective-permute-done | bytes 2080 | tf_op jit(solution)/shard_map/ppermute | solution.py:26
  (73 shorter events, 12.8 us)
Async XLA Ops:
  0.6 9.4 %copy-start = (f32[1,4,128,256]{3,2,1,0:T(8,128)S(1)}, f32[1,4,128,256]{3,2,1,0:T(8,128)}, u32[]{:S(2)}) copy-start(f32[1,4,128,256]{3,2,1,0:T(8,128)} %param.10) | copy-start | bytes 1572868
  0.7 14.8 %collective-permute-start.2 = (f32[1,1,128,128]{2,1,3,0:T(1,128)S(1)}, f32[1,1,128,128]{2,1,3,0:T(1,128)S(1)}, u32[]{:S(2)}, u32[]{:S(2)}) collective-permute-start(f32[1,1,128,128]{2,1,3,0:T(1,128)S(1)} %broadcast.138), channel_id=1, source_target_pairs={{1,0},{2,1},{3,2},{5,4},{6,5},{7,6},{9,8},{10,9},{11,10},{13,12},{... | collective-permute-start | bytes 196616 | tf_op jit(solution)/shard_map/ppermute | solution.py:27
  2.1 13.4 %collective-permute-start.1 = (f32[1,1,128,128]{2,1,3,0:T(1,128)S(1)}, f32[1,1,128,128]{2,1,3,0:T(1,128)S(1)}, u32[]{:S(2)}, u32[]{:S(2)}) collective-permute-start(f32[1,1,128,128]{2,1,3,0:T(1,128)S(1)} %broadcast.138), channel_id=1, source_target_pairs={{0,1},{1,2},{2,3},{4,5},{5,6},{6,7},{8,9},{9,10},{10,11},{12,13},{... | collective-permute-start | bytes 196616 | tf_op jit(solution)/shard_map/ppermute | solution.py:26
  7.8 1.7 %copy-start.1 = (f32[1,4,128,256]{3,2,1,0:T(8,128)S(1)}, f32[1,4,128,256]{3,2,1,0:T(8,128)}, u32[]{:S(2)}) copy-start(f32[1,4,128,256]{3,2,1,0:T(8,128)} %param.11) | copy-start | bytes 1572868
  8.0 6.2 %collective-permute-start = (f32[1,1,128,128]{2,1,3,0:T(1,128)S(1)}, f32[1,1,128,128]{2,1,3,0:T(1,128)S(1)}, u32[]{:S(2)}, u32[]{:S(2)}) collective-permute-start(f32[1,1,128,128]{2,1,3,0:T(1,128)S(1)} %slice.352), channel_id=1, source_target_pairs={{1,0},{2,1},{3,2},{5,4},{6,5},{7,6},{9,8},{10,9},{11,10},{13,12},{... | collective-permute-start | bytes 196616 | tf_op jit(solution)/shard_map/ppermute | solution.py:16
  10.0 1.0 copy-start.6
  11.0 0.9 copy-start.7
  11.9 0.9 copy-start.8
  15.1 22.7 %copy-start.2 = (f32[1,6,128,128]{2,1,3,0:T(8,128)}, f32[1,6,128,128]{2,1,3,0:T(8,128)S(1)}, u32[]{:S(2)}) copy-start(f32[1,6,128,128]{2,1,3,0:T(8,128)S(1)} %get-tuple-element.27) | copy-start | bytes 1179652
  15.1 22.7 %copy-start.4 = (f32[1,6,128,128]{2,1,3,0:T(8,128)}, f32[1,6,128,128]{2,1,3,0:T(8,128)S(1)}, u32[]{:S(2)}) copy-start(f32[1,6,128,128]{2,1,3,0:T(8,128)S(1)} %get-tuple-element.28) | copy-start | bytes 1179652
  16.7 5.4 %collective-permute-start.3 = (f32[1,1,128,128]{2,1,3,0:T(1,128)S(1)}, f32[1,1,128,128]{2,1,3,0:T(1,128)S(1)}, u32[]{:S(2)}, u32[]{:S(2)}) collective-permute-start(f32[1,1,128,128]{2,1,3,0:T(1,128)S(1)} %get-tuple-element.25), channel_id=1, source_target_pairs={{0,1},{1,2},{2,3},{4,5},{5,6},{6,7},{8,9},{9,10},{10,11},{12,13},{... | collective-permute-start | bytes 196616 | tf_op jit(solution)/shard_map/ppermute | solution.py:26
  20.2 6.2 %collective-permute-start.4 = (f32[1,1,128,128]{2,1,3,0:T(1,128)S(1)}, f32[1,1,128,128]{2,1,3,0:T(1,128)S(1)}, u32[]{:S(2)}, u32[]{:S(2)}) collective-permute-start(f32[1,1,128,128]{2,1,3,0:T(1,128)S(1)} %get-tuple-element.26), channel_id=1, source_target_pairs={{1,0},{2,1},{3,2},{5,4},{6,5},{7,6},{9,8},{10,9},{11,10},{13,12},{... | collective-permute-start | bytes 196616 | tf_op jit(solution)/shard_map/ppermute | solution.py:27
  27.3 5.4 %collective-permute-start.5 = (f32[1,1,128,128]{2,1,3,0:T(1,128)S(1)}, f32[1,1,128,128]{2,1,3,0:T(1,128)S(1)}, u32[]{:S(2)}, u32[]{:S(2)}) collective-permute-start(f32[1,1,128,128]{2,1,3,0:T(1,128)S(1)} %get-tuple-element.23), channel_id=1, source_target_pairs={{0,1},{1,2},{2,3},{4,5},{5,6},{6,7},{8,9},{9,10},{10,11},{12,13},{... | collective-permute-start | bytes 196616 | tf_op jit(solution)/shard_map/ppermute | solution.py:26
  30.8 6.2 %collective-permute-start.6 = (f32[1,1,128,128]{2,1,3,0:T(1,128)S(1)}, f32[1,1,128,128]{2,1,3,0:T(1,128)S(1)}, u32[]{:S(2)}, u32[]{:S(2)}) collective-permute-start(f32[1,1,128,128]{2,1,3,0:T(1,128)S(1)} %get-tuple-element.24), channel_id=1, source_target_pairs={{1,0},{2,1},{3,2},{5,4},{6,5},{7,6},{9,8},{10,9},{11,10},{13,12},{... | collective-permute-start | bytes 196616 | tf_op jit(solution)/shard_map/ppermute | solution.py:27
  50.4 7.8 %collective-permute-start.8 = (f32[1,2,256]{2,1,0:T(2,128)S(1)}, f32[1,2,256]{2,1,0:T(2,128)S(1)}, u32[]{:S(2)}, u32[]{:S(2)}) collective-permute-start(f32[1,2,256]{2,1,0:T(2,128)S(1)} %bitcast.117), channel_id=1, source_target_pairs={{4,0},{8,4},{12,8},{16,12},{20,16},{24,20},{28,24},{5,1},{9,5},{13... | collective-permute-start | bytes 6152 | tf_op jit(solution)/shard_map/ppermute | solution.py:27
  52.4 5.9 %collective-permute-start.7 = (f32[1,2,256]{2,1,0:T(2,128)S(1)}, f32[1,2,256]{2,1,0:T(2,128)S(1)}, u32[]{:S(2)}, u32[]{:S(2)}) collective-permute-start(f32[1,2,256]{2,1,0:T(2,128)S(1)} %bitcast.118), channel_id=1, source_target_pairs={{0,4},{4,8},{8,12},{12,16},{16,20},{20,24},{24,28},{1,5},{5,9},{9,... | collective-permute-start | bytes 6152 | tf_op jit(solution)/shard_map/ppermute | solution.py:26
  54.9 4.5 %collective-permute-start.9 = (f32[1,1,128,128]{2,1,3,0:T(1,128)S(1)}, f32[1,1,128,128]{2,1,3,0:T(1,128)S(1)}, u32[]{:S(2)}, u32[]{:S(2)}) collective-permute-start(f32[1,1,128,128]{2,1,3,0:T(1,128)S(1)} %get-tuple-element.21), channel_id=1, source_target_pairs={{0,1},{1,2},{2,3},{4,5},{5,6},{6,7},{8,9},{9,10},{10,11},{12,13},{... | collective-permute-start | bytes 196616 | tf_op jit(solution)/shard_map/ppermute | solution.py:26
  56.9 6.7 %collective-permute-start.10 = (f32[1,1,128,128]{2,1,3,0:T(1,128)S(1)}, f32[1,1,128,128]{2,1,3,0:T(1,128)S(1)}, u32[]{:S(2)}, u32[]{:S(2)}) collective-permute-start(f32[1,1,128,128]{2,1,3,0:T(1,128)S(1)} %get-tuple-element.22), channel_id=1, source_target_pairs={{1,0},{2,1},{3,2},{5,4},{6,5},{7,6},{9,8},{10,9},{11,10},{13,12},{... | collective-permute-start | bytes 196616 | tf_op jit(solution)/shard_map/ppermute | solution.py:27
  58.3 5.4 %copy-start.3 = (f32[1,6,128,128]{2,1,3,0:T(8,128)S(1)}, f32[1,6,128,128]{2,1,3,0:T(8,128)}, u32[]{:S(2)}) copy-start(f32[1,6,128,128]{2,1,3,0:T(8,128)} %copy-done.2) | copy-start | bytes 1179652
  58.3 5.4 %copy-start.5 = (f32[1,6,128,128]{2,1,3,0:T(8,128)S(1)}, f32[1,6,128,128]{2,1,3,0:T(8,128)}, u32[]{:S(2)}) copy-start(f32[1,6,128,128]{2,1,3,0:T(8,128)} %copy-done.4) | copy-start | bytes 1179652
  64.7 5.2 %collective-permute-start.11 = (f32[1,1,128,128]{2,1,3,0:T(1,128)S(1)}, f32[1,1,128,128]{2,1,3,0:T(1,128)S(1)}, u32[]{:S(2)}, u32[]{:S(2)}) collective-permute-start(f32[1,1,128,128]{2,1,3,0:T(1,128)S(1)} %get-tuple-element.17), channel_id=1, source_target_pairs={{0,1},{1,2},{2,3},{4,5},{5,6},{6,7},{8,9},{9,10},{10,11},{12,13},{... | collective-permute-start | bytes 196616 | tf_op jit(solution)/shard_map/ppermute | solution.py:26
  68.0 6.2 %collective-permute-start.12 = (f32[1,1,128,128]{2,1,3,0:T(1,128)S(1)}, f32[1,1,128,128]{2,1,3,0:T(1,128)S(1)}, u32[]{:S(2)}, u32[]{:S(2)}) collective-permute-start(f32[1,1,128,128]{2,1,3,0:T(1,128)S(1)} %get-tuple-element.18), channel_id=1, source_target_pairs={{1,0},{2,1},{3,2},{5,4},{6,5},{7,6},{9,8},{10,9},{11,10},{13,12},{... | collective-permute-start | bytes 196616 | tf_op jit(solution)/shard_map/ppermute | solution.py:27
  75.1 4.1 %collective-permute-start.13 = (f32[1,1,128,128]{2,1,3,0:T(1,128)S(1)}, f32[1,1,128,128]{2,1,3,0:T(1,128)S(1)}, u32[]{:S(2)}, u32[]{:S(2)}) collective-permute-start(f32[1,1,128,128]{2,1,3,0:T(1,128)S(1)} %get-tuple-element.15), channel_id=1, source_target_pairs={{0,1},{1,2},{2,3},{4,5},{5,6},{6,7},{8,9},{9,10},{10,11},{12,13},{... | collective-permute-start | bytes 196616 | tf_op jit(solution)/shard_map/ppermute | solution.py:26
  77.3 6.2 %collective-permute-start.14 = (f32[1,1,128,128]{2,1,3,0:T(1,128)S(1)}, f32[1,1,128,128]{2,1,3,0:T(1,128)S(1)}, u32[]{:S(2)}, u32[]{:S(2)}) collective-permute-start(f32[1,1,128,128]{2,1,3,0:T(1,128)S(1)} %get-tuple-element.16), channel_id=1, source_target_pairs={{1,0},{2,1},{3,2},{5,4},{6,5},{7,6},{9,8},{10,9},{11,10},{13,12},{... | collective-permute-start | bytes 196616 | tf_op jit(solution)/shard_map/ppermute | solution.py:27
  96.9 5.2 %collective-permute-start.16 = (f32[1,2,256]{2,1,0:T(2,128)S(1)}, f32[1,2,256]{2,1,0:T(2,128)S(1)}, u32[]{:S(2)}, u32[]{:S(2)}) collective-permute-start(f32[1,2,256]{2,1,0:T(2,128)S(1)} %bitcast.114), channel_id=1, source_target_pairs={{4,0},{8,4},{12,8},{16,12},{20,16},{24,20},{28,24},{5,1},{9,5},{13... | collective-permute-start | bytes 6152 | tf_op jit(solution)/shard_map/ppermute | solution.py:27
  98.8 5.8 %collective-permute-start.15 = (f32[1,2,256]{2,1,0:T(2,128)S(1)}, f32[1,2,256]{2,1,0:T(2,128)S(1)}, u32[]{:S(2)}, u32[]{:S(2)}) collective-permute-start(f32[1,2,256]{2,1,0:T(2,128)S(1)} %bitcast.115), channel_id=1, source_target_pairs={{0,4},{4,8},{8,12},{12,16},{16,20},{20,24},{24,28},{1,5},{5,9},{9,... | collective-permute-start | bytes 6152 | tf_op jit(solution)/shard_map/ppermute | solution.py:26
